TPU v7x, 32 devices: a whole 2x2x4 slice. The times are simulated.
32 devices in a mesh: context: 8 (over z, core), expert: 4 (over y, x).
Axes of the slice: x: 2, y: 2, z: 4, core: 2. Of those that a mesh axis runs over, the one named last changes fastest.
Arguments:
- residual: bfloat16 [2048, 6144], P(('context', 'expert')), may hold values from -6 to 6
- attn_queries: bfloat16 [2048, 8192], P('context', 'expert'), may hold values from -6 to 6
- attn_keys: bfloat16 [2048, 8192], P('context', 'expert'), may hold values from -0.5 to 0.5
- attn_values: bfloat16 [2048, 8192], P('context', 'expert'), may hold values from -6 to 6
- decay_rate: float32 [64, 2048], P('expert', 'context'), may hold values from 0 to 1, as said below
- start_state: float32 [64, 128, 128], P('expert'), may hold values from -12 to 12
- out_proj: bfloat16 [8192, 6144], P('expert', 'context'), may hold values from -0.0625 to 0.0625
- moe_gain: float32 [6144], replicated, may hold values from 0.5 to 1.5
- gate_proj: bfloat16 [4, 6144, 4608], P('expert', None, 'context'), may hold values from -0.078125 to 0.078125
- up_proj: bfloat16 [4, 6144, 4608], P('expert', None, 'context'), may hold values from -0.078125 to 0.078125
- down_proj: bfloat16 [4, 4608, 6144], P('expert', None, 'context'), may hold values from -0.09375 to 0.09375
- expert_ids: int32 [2048, 2], P(('context', 'expert')), may hold values from 0 to 3, all different within a row; in each aligned block of 64 rows (0 to 63, 64 to 127, ...) at most 48 rows name the same one
- expert_gates: float32 [2048, 2], P(('context', 'expert')), may hold values from 0.25 to 1
Outputs:
- layer_out: bfloat16 [2048, 6144], P(('context', 'expert'))
Inputs may be any that keep to these rules, and one draw needn't show every extreme that they name: `decay_rate`: non-negative rates. `expert_ids`: each row names two different experts; among the 64 rows of one aligned block no expert is named by more than 48 rows.
All inputs are finite; a program needn't handle non-finite values.
Results may differ from a plain program's by a relative error of at most 0.015.
Values may be sent and summed in bfloat16 or wider, within the bound.
No kernel may reach another device: no remote copies, remote signals or barrier semaphores. Data moves between devices by JAX's collectives and lax.ppermute only.
A program may use at most 192 MiB of HBM per device.

v0:
```python
import jax
import jax.numpy as jnp
from jax import lax
from jax.sharding import PartitionSpec as P


def carried_in(x, axis, combine, identity):
    count, place = (lax.axis_size(axis), lax.axis_index(axis))
    everything = jax.tree.map(
        lambda part, kind: lax.all_gather(part.astype(kind), axis), x, (jnp.bfloat16, jnp.bfloat16)
    )
    start = jax.tree.map(
        lambda part, zero: jnp.broadcast_to(jnp.asarray(zero, part.dtype), part.shape), x, identity
    )

    def step(k, before):
        reached = k < place
        new = combine(
            before, jax.tree.map(lambda part, own: part[k].astype(own.dtype), everything, x)
        )
        return jax.tree.map(lambda a, b: jnp.where(reached, a, b), new, before)

    return lax.fori_loop(0, count, step, start)


def link_states(earlier, later):
    return (earlier[0] + later[0], jnp.exp(-later[0])[:, None, None] * earlier[1] + later[1])


def shards(
    residual,
    attn_queries,
    attn_keys,
    attn_values,
    decay_rate,
    start_state,
    out_proj,
    moe_gain,
    gate_proj,
    up_proj,
    down_proj,
    expert_ids,
    expert_gates,
):
    n_ctx = lax.axis_size("context")
    n_exp = lax.axis_size("expert")
    heads = start_state.shape[0]
    head_dim = start_state.shape[1]
    length = attn_queries.shape[0]
    queries = attn_queries.reshape(length, heads, head_dim)
    keys_in = attn_keys.reshape(length, heads, head_dim)
    values_in = attn_values.reshape(length, heads, head_dim)
    cum = jnp.cumsum(decay_rate, axis=1)
    total = cum[:, -1]
    positions = jnp.arange(length)
    causal = (positions[None, :] <= positions[:, None])[None, :, :]
    diff = cum[:, None, :] - cum[:, :, None]
    decay = jnp.where(causal, jnp.exp(jnp.where(causal, diff, 0.0)), 0.0)
    scores = jnp.einsum("thd,shd->hts", queries, keys_in, preferred_element_type=jnp.float32)
    weights = (scores * decay).astype(jnp.bfloat16)
    intra = jnp.einsum("hts,shd->thd", weights, values_in, preferred_element_type=jnp.float32)
    scaled_keys = keys_in.astype(jnp.float32) * jnp.exp(cum - total[:, None]).T[:, :, None]
    local = jnp.einsum(
        "shd,she->hde", scaled_keys, values_in.astype(jnp.float32), precision=lax.Precision.HIGHEST
    )
    before_decay, before_state = carried_in(
        (total, local), "context", link_states, (jnp.zeros_like(total), jnp.zeros_like(local))
    )
    incoming = jnp.exp(-before_decay)[:, None, None] * start_state + before_state
    inter = jnp.einsum(
        "thd,hde->the", queries.astype(jnp.float32), incoming, precision=lax.Precision.HIGHEST
    )
    attended = intra + inter * jnp.exp(-cum).T[:, :, None]
    scale = lax.rsqrt(jnp.mean(attended * attended, axis=-1, keepdims=True) + 1e-06)
    head_out = (attended * scale).astype(jnp.bfloat16).reshape(length, heads * head_dim)
    partial_rows = jnp.dot(
        head_out,
        lax.all_gather(out_proj, "context", axis=1, tiled=True),
        preferred_element_type=jnp.float32,
    )
    projected = lax.psum_scatter(
        partial_rows.astype(jnp.bfloat16), "expert", scatter_dimension=0, tiled=True
    ).astype(jnp.float32)
    stream = (residual.astype(jnp.float32) + projected).astype(jnp.bfloat16)
    stream32 = stream.astype(jnp.float32)
    moe_in = (
        stream32
        * lax.rsqrt(jnp.mean(stream32 * stream32, axis=-1, keepdims=True) + 1e-06)
        * moe_gain
    ).astype(jnp.bfloat16)
    rows = residual.shape[0]
    width = residual.shape[1]
    capacity = 3 * rows // n_exp
    flat_ids = expert_ids.reshape(-1)
    onehot = (flat_ids[:, None] == jnp.arange(n_exp)[None, :]).astype(jnp.int32)
    slot = jnp.sum((jnp.cumsum(onehot, axis=0) - 1) * onehot, axis=1)
    target = flat_ids * capacity + slot
    picks = (target[:, None] == jnp.arange(n_exp * capacity)[None, :]).astype(jnp.bfloat16)
    placing = picks.reshape(rows, 2, n_exp * capacity).sum(axis=1)
    w_gate = gate_proj[0]
    w_up = up_proj[0]
    w_down = down_proj[0]
    outgoing = jnp.einsum("tr,td->rd", placing, moe_in, preferred_element_type=jnp.float32).astype(
        jnp.bfloat16
    )
    outgoing = outgoing.reshape(n_exp, capacity, width)
    arrived = lax.all_to_all(outgoing, "expert", split_axis=0, concat_axis=0, tiled=True)
    block = lax.all_gather(arrived, "context", axis=0, tiled=True)
    flat = block.reshape(-1, block.shape[-1])
    gate = jnp.dot(flat, w_gate, preferred_element_type=jnp.float32)
    upper = jnp.dot(flat, w_up, preferred_element_type=jnp.float32)
    hidden = (jax.nn.silu(gate) * upper).astype(jnp.bfloat16)
    hidden_all = hidden.reshape(block.shape[:-1] + (w_gate.shape[1],))
    hidden_all = hidden_all.reshape(n_ctx, n_exp, capacity, w_gate.shape[1])
    block = w_down
    expert_out = jnp.einsum(
        "abcf,fd->abcd",
        lax.all_gather(hidden_all, "context", axis=3, tiled=True),
        block,
        preferred_element_type=jnp.float32,
    ).astype(jnp.bfloat16)
    returned = lax.all_to_all(
        lax.all_to_all(expert_out, "context", split_axis=0, concat_axis=3, tiled=True),
        "expert",
        split_axis=1,
        concat_axis=1,
        tiled=True,
    )
    chosen = jnp.dot(
        picks, returned.reshape(n_exp * capacity, width), preferred_element_type=jnp.float32
    )
    mixture = jnp.sum(chosen.reshape(rows, 2, width) * expert_gates[:, :, None], axis=1)
    return (stream32 + mixture).astype(jnp.bfloat16)


def solution(mesh):
    placed = (
        P(("context", "expert"), None),
        P("context", "expert"),
        P("context", "expert"),
        P("context", "expert"),
        P("expert", "context"),
        P("expert", None, None),
        P("expert", "context"),
        P(),
        P("expert", None, "context"),
        P("expert", None, "context"),
        P("expert", None, "context"),
        P(("context", "expert"), None),
        P(("context", "expert"), None),
    )
    return jax.shard_map(
        shards,
        mesh=mesh,
        in_specs=placed,
        out_specs=P(("context", "expert"), None),
        check_vma=False,
    )
```

profile of v0, /device:TPU:0, one launch (start us, length us, event | category | flops | bytes accessed | tf_op | source)
XLA Modules:
  0.0 1028.3 jit_solution(15532580775604200535)
XLA Ops:
  6.5 0.8 copy_bitcast_fusion.1
  7.3 0.6 reduce-window.6
  7.9 0.2 slice_reduce_fusion
  8.1 0.1 copy_bitcast_fusion
  8.2 0.2 slice_reduce_fusion.1
  8.4 0.1 exponential_bitcast_fusion.1
  8.5 1.5 copy.112
  10.0 3.3 fusion.30
  13.3 0.0 all-gather.13.cloned.1.call-update
  13.3 0.0 all-gather.7.cloned.1.call-start
  13.3 0.7 all-gather.7.cloned.1.call-update
  14.0 0.0 reduce-scatter.2.cloned.1.call-start
  14.1 0.6 dynamic-slice
  15.5 0.2 fusion.56
  15.6 0.2 dynamic-update-slice
  15.9 18.4 %all-reduce = bf16[128]{0:T(256)(128)(2,1)S(1)} all-reduce(bf16[128]{0:T(256)(128)(2,1)S(1)} %dynamic-update-slice), channel_id=2, replica_groups=mesh['context'=8,'expert'=4] {'context'}, use_global_device_ids=true, to_apply=%add | all-reduce | flops 128 | bytes 512
  34.3 0.1 reshape.166
  34.4 4.4 fusion.29
  38.8 24.6 %all-gather.13.cloned.1.call-done = bf16[128,128,128]{2,1,0:T(8,128)(2,1)} async-done(((bf16[16,128,128]{2,1,0:T(8,128)(2,1)}), bf16[128,128,128]{2,1,0:T(8,128)(2,1)}) %all-gather.13.cloned.1.call-update) | async-done | bytes 4194320 | tf_op jit(solution)/shard_map/all_gather | solution.py:10
  63.4 11.0 %while.16 = (s32[]{:T(128)}, f32[16]{0:T(128)S(1)}, f32[16,128,128]{2,1,0:T(8,128)S(1)}, s32[]{:T(128)}, bf16[8,16]{1,0:T(8,128)(2,1)S(1)}, /*index=5*/bf16[8,16,128,128]{3,2,1,0:T(8,128)(2,1)}, s32[]{:T(128)}, s32[]{:T(128)}) while((s32[]{:T(128)}, f32[16]{0:T(128)S(1)}, f32[16,128,128]{2,1,0:T(8,128)S(1)}, s32[]{:T(128)}, ...), condition=%wide.region_3.4_spmd.clone, body=%wide.region_2.3_spmd.clone.sunk | while | flops 1310804 | bytes 2621851 | solution.py:23
  63.4 1.4 fusion.73
  64.8 1.3 fusion.73
  66.1 1.3 fusion.73
  67.5 1.3 fusion.73
  68.8 1.3 fusion.73
  70.1 1.4 fusion.73
  71.6 1.4 fusion.73
  73.0 1.4 fusion.73
  74.4 3.4 multiply_reduce_fusion
  77.8 0.2 multiply_convert_fusion.1
  78.0 205.8 %all-gather.7.cloned.1.call-done = bf16[2048,6144]{1,0:T(8,128)(2,1)} async-done(((bf16[2048,768]{1,0:T(8,128)(2,1)}), bf16[2048,6144]{1,0:T(8,128)(2,1)}) %all-gather.7.cloned.1.call-update) | async-done | bytes 25165840 | tf_op jit(solution)/shard_map/all_gather | solution.py:78
  283.9 12.8 %convolution_convert_fusion = bf16[256,6144]{1,0:T(8,128)(2,1)} fusion(bf16[256,2048]{0,1:T(8,128)(2,1)S(1)} %bitcast.115, bf16[2048,6144]{1,0:T(8,128)(2,1)} %all-gather.7.cloned.1.call-done), kind=kOutput, calls=%fused_computation.9 | convolution fusion | flops 6444023808 | bytes 29360128 | tf_op jit(solution)/shard_map/dot_general | solution.py:76
  296.7 0.0 reduce-scatter.2.cloned.1.call-update
  296.7 0.0 all-gather.9.cloned.1.call-start
  296.8 0.6 copy-done.8
  297.4 0.1 copy.103
  297.5 0.1 eq.51
  297.6 0.1 fusion.55
  297.7 0.2 reduce_window_sum.36
  297.9 0.2 select_reduce_fusion
  298.1 0.1 reduce_sum.52
  298.2 0.1 copy.104
  298.3 0.1 fusion.53
  298.4 40.6 %reduce-scatter.2.cloned.1.call-done = bf16[64,6144]{1,0:T(8,128)(2,1)} async-done(((bf16[256,6144]{1,0:T(8,128)(2,1)}), bf16[64,6144]{1,0:T(8,128)(2,1)}) %reduce-scatter.2.cloned.1.call-update) | async-done | bytes 786448 | tf_op jit(solution)/shard_map/reduce_scatter | solution.py:81
  339.0 1.5 fusion.25
  340.6 2.0 convolution_convert_fusion.1
  342.5 31.7 %all_to_all.28 = bf16[4,48,6144]{2,1,0:T(8,128)(2,1)} all-to-all(bf16[4,48,6144]{2,1,0:T(8,128)(2,1)S(1)} %bitcast.110), channel_id=1, replica_groups=mesh['context'=8,'expert'=4] {'expert'}, dimensions={0} | all-to-all | bytes 4718592 | tf_op jit(solution)/shard_map/all_to_all | solution.py:107
  374.2 0.0 all-gather.9.cloned.1.call-update
  374.3 0.2 all-gather.11.cloned.1.call-start
  374.5 167.7 %all-gather.9.cloned.1.call-done = bf16[32,48,6144]{2,1,0:T(8,128)(2,1)} async-done(((bf16[4,48,6144]{2,1,0:T(8,128)(2,1)}), bf16[32,48,6144]{2,1,0:T(8,128)(2,1)}) %all-gather.9.cloned.1.call-update) | async-done | bytes 18874384 | tf_op jit(solution)/shard_map/all_gather | solution.py:108
  542.2 16.1 %fusion.7 = f32[1536,576]{0,1:T(8,128)S(1)} fusion(bf16[1536,6144]{1,0:T(8,128)(2,1)} %bitcast.119, bf16[1,6144,576]{1,2,0:T(8,128)(2,1)} %param.23), kind=kOutput, calls=%fused_computation.15 | convolution fusion | flops 10871635968 | bytes 29491200 | tf_op jit(solution)/shard_map/dot_general | solution.py:110
  558.3 18.3 %fusion.12 = bf16[1536,576]{0,1:T(8,128)(2,1)} fusion(bf16[1536,6144]{1,0:T(8,128)(2,1)} %bitcast.120, bf16[1,6144,576]{1,2,0:T(8,128)(2,1)} %param.24, f32[1536,576]{0,1:T(8,128)S(1)} %fusion.7), kind=kOutput, calls=%fused_computation.19 | convolution fusion | flops 10876944384 | bytes 31260672 | tf_op jit(solution)/shard_map/dot_general | solution.py:111
  576.6 2.7 copy.105
  579.3 7.8 copy.106
  587.1 0.0 all-gather.11.cloned.1.call-update
  587.1 322.9 %all-gather.11.cloned.1.call-done = bf16[8,4,48,4608]{2,0,1,3:T(8,128)(2,1)} async-done(((bf16[8,4,48,576]{2,0,1,3:T(8,128)(2,1)}), bf16[8,4,48,4608]{2,0,1,3:T(8,128)(2,1)}) %all-gather.11.cloned.1.call-update) | async-done | bytes 14155792 | tf_op jit(solution)/shard_map/all_gather | solution.py:118
  910.0 20.6 %fusion.19 = bf16[8,4,48,768]{3,2,1,0:T(8,128)(2,1)S(1)} fusion(bf16[1,4608,768]{2,1,0:T(8,128)(2,1)} %param.25, bf16[8,4,48,4608]{2,0,1,3:T(8,128)(2,1)} %all-gather.11.cloned.1.call-done), kind=kOutput, calls=%fused_computation.30 | convolution fusion | flops 10872815616 | bytes 23592960 | tf_op jit(solution)/shard_map/abcf,fd->abcd/dot_general | solution.py:116
  930.6 57.1 %all_to_all.29 = bf16[8,4,48,768]{3,2,1,0:T(8,128)(2,1)S(1)} all-to-all(bf16[8,4,48,768]{3,2,1,0:T(8,128)(2,1)S(1)} %fusion.19), channel_id=1, replica_groups=mesh['context'=8,'expert'=4] {'context'}, dimensions={0} | all-to-all | bytes 4718592 | tf_op jit(solution)/shard_map/all_to_all | solution.py:123
  987.7 0.3 copy.117
  988.0 31.3 %all_to_all.30 = bf16[1,4,48,6144]{3,2,0,1:T(8,128)(2,1)S(1)} all-to-all(bf16[1,4,48,6144]{3,2,0,1:T(8,128)(2,1)S(1)} %bitcast.113), channel_id=1, replica_groups=mesh['context'=8,'expert'=4] {'expert'}, dimensions={1} | all-to-all | bytes 4718592 | tf_op jit(solution)/shard_map/all_to_all | solution.py:122
  1019.3 0.7 fusion.24
  1020.0 0.4 copy-done.3
  1020.4 0.2 copy-done.4
  1020.7 1.1 fusion.28
  (36 shorter events, 0.3 us)
Async XLA Ops:
  6.5 27.9 %copy-start = (bf16[256,2048]{1,0:T(8,128)(2,1)S(1)}, bf16[256,2048]{1,0:T(8,128)(2,1)}, u32[]{:S(2)}) copy-start(bf16[256,2048]{1,0:T(8,128)(2,1)} %param.16) | copy-start | bytes 3145732
  6.5 56.8 %all-gather.13.cloned.1.call-start = ((), (), s32[]{:S(2)}) async-start(), calls=%async_computation.8 | async-start | bytes 4718592 | tf_op jit(solution)/shard_map/all_gather | solution.py:10
  10.0 4.2 copy-start.9
  13.3 270.6 %all-gather.7.cloned.1.call-start = ((), (), s32[]{:S(2)}) async-start(), calls=%async_computation.4 | async-start | bytes 28311552 | tf_op jit(solution)/shard_map/all_gather | solution.py:78
  14.0 325.0 %reduce-scatter.2.cloned.1.call-start = ((), (), s32[]{:S(2)}) async-start(), calls=%async_computation.5 | async-start | bytes 3932160 | tf_op jit(solution)/shard_map/reduce_scatter | solution.py:81
  63.4 11.0 %copy-start.5 = (f32[16,128,128]{2,1,0:T(8,128)S(1)}, f32[16,128,128]{2,1,0:T(8,128)}, u32[]{:S(2)}) copy-start(f32[16,128,128]{2,1,0:T(8,128)} %param.20) | copy-start | bytes 3145732
  296.7 0.7 copy-start.8
  296.7 42.3 %copy-start.2 = (bf16[64,6144]{1,0:T(8,128)(2,1)S(1)}, bf16[64,6144]{1,0:T(8,128)(2,1)}, u32[]{:S(2)}) copy-start(bf16[64,6144]{1,0:T(8,128)(2,1)} %param.15) | copy-start | bytes 2359300
  296.7 43.8 %copy-start.6 = (f32[6144]{0:T(1024)S(1)}, f32[6144]{0:T(1024)}, u32[]{:S(2)}) copy-start(f32[6144]{0:T(1024)} %param.22) | copy-start | bytes 73732
  296.7 245.4 %all-gather.9.cloned.1.call-start = ((), (), s32[]{:S(2)}) async-start(), calls=%async_computation.6 | async-start | bytes 21233664 | tf_op jit(solution)/shard_map/all_gather | solution.py:108
  374.3 535.7 %all-gather.11.cloned.1.call-start = ((), (), s32[]{:S(2)}) async-start(), calls=%async_computation.7 | async-start | bytes 42467328 | tf_op jit(solution)/shard_map/all_gather | solution.py:118
  988.0 31.3 %copy-start.7 = (f32[64,2]{0,1:T(2,128)S(1)}, f32[64,2]{0,1:T(2,128)}, u32[]{:S(2)}) copy-start(f32[64,2]{0,1:T(2,128)} %param.27) | copy-start | bytes 1540
  1019.3 1.1 copy-start.3
  1019.3 1.4 copy-start.4
  1019.3 2.5 copy-start.1
Sparse Core Ops, SparseCore 0:
  13.4 49.9 all-gather.12
  65.0 218.8 all-gather.6
  296.9 42.1 reduce-scatter.1
  374.4 167.7 all-gather.8
  587.2 322.7 all-gather.10
where the time goes:
time: 1030 us
  waiting for transfers between devices  762 us (74%)
  blocking collectives  139 us (13%)
  matrix products  81.5 us (8%)
  local copies, waits for them, and re-layouts  16.3 us (2%)
  other arithmetic  15 us (1%)
  between operations  14.1 us (1%)
    all_gather x1, waiting for transfers between devices, shards(): lax.all_gather(hidden_all, 'context', axis=3, tiled=True)  323 us
    all_gather x1, waiting for transfers between devices, shards(): lax.all_gather(out_proj, 'context', axis=1, tiled=True)  206 us
    all_gather x1, waiting for transfers between devices, shards(): block = lax.all_gather(arrived, 'context', axis=0, tiled=True)  168 us
    all_to_all x1, blocking collectives, shards(): lax.all_to_all(expert_out, 'context', split_axis=0, concat_axis=3, tiled=...  57.1 us
    reduce_scatter x1, waiting for transfers between devices, shards(): lax.psum_scatter(partial_rows.astype(jnp.bfloat16), 'expert', scatter_dim...  40.6 us
    all_to_all x1, blocking collectives, shards(): lax.all_to_all(outgoing, 'expert', split_axis=0, concat_axis=0, tiled=True)  31.7 us
    all_to_all x1, blocking collectives, shards(): lax.all_to_all(lax.all_to_all(expert_out, 'context', split_axis=0, concat...  31.3 us
    all_gather x1, waiting for transfers between devices, carried_in(): lax.all_gather(part.astype(kind), axis)  24.6 us
  transfers between devices with their start and end apart: 5, of which 5 were waited for; matrix products, arithmetic and copies ran while one was open for 2% of the time, Pallas kernels for 0%

commit v1 on v0

v1 whole, which is shorter than its diff:
```python
import jax
import jax.numpy as jnp
from jax import lax
from jax.sharding import Mesh
from jax.sharding import PartitionSpec as P

BF = jnp.bfloat16
F32 = jnp.float32


def swap_core(x):
    return lax.ppermute(x, "core", [(0, 1), (1, 0)])


def shift_z(x, by, wrap=False):
    n = lax.axis_size("z")
    if wrap:
        perm = [(i, (i + by) % n) for i in range(n)]
    else:
        perm = [(i, i + by) for i in range(n) if 0 <= i + by < n]
    return lax.ppermute(x, "z", perm)


def to_expert(x, k):
    n = lax.axis_size("expert")
    return lax.ppermute(x, "expert", [(i, i ^ k) for i in range(n)])


def by_core(core, own, other):
    first = core == 0
    return jnp.where(first, own, other), jnp.where(first, other, own)


def line_gather(x):
    n = lax.axis_size("z")
    z = lax.axis_index("z")
    right, left = [x], [x]
    for _ in range(n - 1):
        right.append(shift_z(right[-1], 1))
        left.append(shift_z(left[-1], -1))
    return [x] + [jnp.where(z >= k, right[k], left[n - k]) for k in range(1, n)]


def absolute(pieces, axis):
    n = len(pieces)
    z = lax.axis_index("z")
    stacked = jnp.stack(pieces)
    return jnp.concatenate(
        [
            lax.dynamic_index_in_dim(stacked, lax.rem(z - s + n, n), 0, keepdims=False)
            for s in range(n)
        ],
        axis=axis,
    )


def attention(queries, keys, values, decay_rate, start_state):
    core, z, n_z = lax.axis_index("core"), lax.axis_index("z"), lax.axis_size("z")
    heads, head_dim = start_state.shape[:2]
    length = queries.shape[0]
    queries = queries.reshape(length, heads, head_dim)
    keys = keys.reshape(length, heads, head_dim)
    values = values.reshape(length, heads, head_dim)
    positions = jnp.arange(length)
    upto = positions[:, None] <= positions[None, :]
    cum = jnp.dot(decay_rate, upto.astype(F32), precision=lax.Precision.HIGHEST)
    total = cum[:, -1]
    scaled_keys = keys.astype(F32) * jnp.exp(cum - total[:, None]).T[:, :, None]
    local = jnp.einsum(
        "shd,she->hde", scaled_keys, values.astype(F32), precision=lax.Precision.HIGHEST
    )
    other_total, other_local = swap_core(total), swap_core(local.astype(BF)).astype(F32)
    total0, total1 = by_core(core, total, other_total)
    half = heads // 2

    def mine(x):
        return lax.dynamic_slice_in_dim(x, core * half, half, 0)

    own_half, other_half = mine(local), mine(other_local)
    local0, local1 = by_core(core, own_half, other_half)
    chip_total = total0 + total1
    chip_state = (jnp.exp(-mine(total1))[:, None, None] * local0 + local1).astype(BF)
    earlier_states = [shift_z(chip_state, k) for k in range(1, n_z)]
    earlier_totals = [shift_z(chip_total, k) for k in range(1, n_z)]

    causal = upto.T[None, :, :]
    diff = cum[:, None, :] - cum[:, :, None]
    decay = jnp.where(causal, jnp.exp(jnp.where(causal, diff, 0.0)), 0.0)
    scores = jnp.einsum("thd,shd->hts", queries, keys, preferred_element_type=F32)
    weights = (scores * decay).astype(BF)
    intra = jnp.einsum("hts,shd->thd", weights, values, preferred_element_type=F32)

    passed = jnp.zeros_like(total)
    incoming = jnp.zeros((half, head_dim, head_dim), F32)
    for state, decayed in zip(earlier_states, earlier_totals):
        incoming = incoming + jnp.exp(-mine(passed))[:, None, None] * state.astype(F32)
        passed = passed + decayed
    incoming = incoming + jnp.exp(-mine(passed))[:, None, None] * mine(start_state)
    incoming = incoming.astype(BF)
    in0, in1 = by_core(core, incoming, swap_core(incoming))
    incoming = jnp.concatenate([in0, in1], axis=0).astype(F32)
    incoming = jnp.where(
        core == 0, incoming, jnp.exp(-total0)[:, None, None] * incoming + other_local
    )
    inter = jnp.einsum(
        "thd,hde->the", queries.astype(F32), incoming, precision=lax.Precision.HIGHEST
    )
    attended = intra + inter * jnp.exp(-cum).T[:, :, None]
    scale = lax.rsqrt(jnp.mean(attended * attended, axis=-1, keepdims=True) + 1e-06)
    return (attended * scale).astype(BF).reshape(length, heads * head_dim)


def shards(
    residual,
    attn_queries,
    attn_keys,
    attn_values,
    decay_rate,
    start_state,
    out_proj,
    moe_gain,
    gate_proj,
    up_proj,
    down_proj,
    expert_ids,
    expert_gates,
):
    n_z, n_exp = lax.axis_size("z"), lax.axis_size("expert")
    z, core, expert = lax.axis_index("z"), lax.axis_index("core"), lax.axis_index("expert")
    rows, width = residual.shape
    part = width // n_z
    capacity = 3 * rows // n_exp

    w_out = jnp.concatenate(by_core(core, out_proj, swap_core(out_proj)), axis=1)
    gate_t, up_t = gate_proj[0].T, up_proj[0].T
    w_in = jnp.concatenate(
        by_core(core, gate_t, swap_core(gate_t)) + by_core(core, up_t, swap_core(up_t)), axis=0
    )
    down = down_proj[0]
    w_down = jnp.concatenate(by_core(core, down, swap_core(down)), axis=1)

    named = jnp.concatenate([expert_ids.astype(F32), expert_gates], axis=1)
    named = absolute([named[None]] + [shift_z(named[None], k, True) for k in range(1, n_z)], 0)
    ids, gates = named[:, :, :2].astype(jnp.int32), named[:, :, 2:]
    blocks = residual.reshape(rows, n_z, part)

    def columns_of(k):
        return lax.dynamic_index_in_dim(blocks, lax.rem(z + k, n_z), 1, keepdims=False)

    kept = [columns_of(0)] + [shift_z(columns_of(k), k, True) for k in range(1, n_z)]

    partner = expert ^ jnp.arange(n_exp)
    names = ids[:, :, :, None] == partner
    member = jnp.any(names, axis=2)
    before = jnp.arange(rows)[None, :] < jnp.arange(rows)[:, None]
    slot = jnp.einsum(
        "tu,suk->stk", before.astype(BF), member.astype(BF), preferred_element_type=F32
    ).astype(jnp.int32)
    places = jnp.arange(capacity)
    placed = member[:, :, :, None] & (slot[:, :, :, None] == places)
    chosen = names[:, :, :, :, None] & (slot[:, :, None, :, None] == places)
    chosen = chosen.astype(BF).reshape(n_z, rows, 2, n_exp * capacity)

    head_out = attention(attn_queries, attn_keys, attn_values, decay_rate, start_state)
    gathered = jnp.stack(line_gather(head_out)).reshape(n_z, n_exp, rows, -1)

    def projected_for(k):
        block = lax.dynamic_index_in_dim(gathered, expert ^ k, 1, keepdims=False)
        return jnp.einsum("std,df->stf", block, w_out, preferred_element_type=F32).astype(BF)

    summed = jnp.zeros((n_z, rows, part), F32)
    for k in reversed(range(n_exp)):
        piece = projected_for(k)
        summed = summed + (to_expert(piece, k) if k else piece).astype(F32)
    stream = (jnp.stack(kept).astype(F32) + summed).astype(BF)
    stream = absolute(list(stream[:, None]), 0)

    full = absolute(line_gather(stream), 2).astype(F32)
    moe_in = (
        full * lax.rsqrt(jnp.mean(full * full, axis=-1, keepdims=True) + 1e-06) * moe_gain
    ).astype(BF)

    routed = []
    for k in reversed(range(n_exp)):
        block = jnp.einsum(
            "stc,std->scd",
            placed[:, :, k].astype(BF),
            moe_in,
            preferred_element_type=F32,
        ).astype(BF)
        routed.append(to_expert(block, k) if k else block)
    routed = jnp.stack(routed[::-1]).reshape(-1, width)

    pre = jnp.einsum("rd,fd->rf", routed, w_in, preferred_element_type=F32)
    units = pre.shape[1] // 2
    hidden = (jax.nn.silu(pre[:, :units]) * pre[:, units:]).astype(BF)
    w_down = w_down.reshape(n_z, units, part)
    expert_out = jnp.zeros((hidden.shape[0], part), F32)
    for k, piece in enumerate(line_gather(hidden)):
        w = lax.dynamic_index_in_dim(w_down, lax.rem(z - k + n_z, n_z), 0, keepdims=False)
        expert_out = expert_out + jnp.dot(piece, w, preferred_element_type=F32)
    expert_out = expert_out.astype(BF).reshape(n_exp, n_z, capacity, part)

    returned = [to_expert(expert_out[k], k) if k else expert_out[k] for k in range(n_exp)]
    returned = jnp.stack(returned, axis=1).reshape(n_z, n_exp * capacity, part)
    out = stream.astype(F32)
    for j in range(2):
        picked = jnp.einsum("str,srd->std", chosen[:, :, j], returned, preferred_element_type=F32)
        out = out + picked * gates[:, :, j, None]
    out = out.astype(BF)

    def rows_of(k):
        return lax.dynamic_index_in_dim(out, lax.rem(z + k, n_z), 0, keepdims=False)

    return absolute([rows_of(0)] + [shift_z(rows_of(k), k, True) for k in range(1, n_z)], 1)


def solution(mesh):
    n_ctx, n_exp = mesh.shape["context"], mesh.shape["expert"]
    fine = Mesh(mesh.devices.reshape(n_ctx // 2, 2, n_exp), ("z", "core", "expert"))
    ctx = ("z", "core")
    owner = ("z", "core", "expert")
    placed = (
        P(owner, None),
        P(ctx, "expert"),
        P(ctx, "expert"),
        P(ctx, "expert"),
        P("expert", ctx),
        P("expert", None, None),
        P("expert", ctx),
        P(),
        P("expert", None, ctx),
        P("expert", None, ctx),
        P("expert", None, ctx),
        P(owner, None),
        P(owner, None),
    )
    return jax.shard_map(
        shards, mesh=fine, in_specs=placed, out_specs=P(owner, None), check_vma=False
    )
```

time: 1030 us -> 582 us (0.57)
  waiting for transfers between devices: 762 us -> 327 us
  blocking collectives: 139 us -> 0 us
  starting transfers between devices: 0.35 us -> 106 us
  other arithmetic: 15 us -> 37.3 us
  between operations: 14.1 us -> 1.43 us
  matrix products: 81.5 us -> 93.6 us
    all_gather x4 -> x0, waiting for transfers between devices: 721 us -> none  [the longest x1 323 us: shards(): lax.all_gather(hidden_all, 'context', axis=3, tiled=True)]
    ppermute x0 -> x49, waiting for transfers between devices: none -> 327 us  [the longest x33 214 us: shift_z(): return lax.ppermute(x, 'z', perm)]
    all_to_all x3 -> x0, blocking collectives: 120 us -> none  [the longest x1 57.1 us: shards(): lax.all_to_all(expert_out, 'context', split_axis=0, concat_axis=3, tiled=...]
    ppermute x0 -> x49, starting transfers between devices: none -> 106 us  [the longest x33 91.4 us: shift_z(): return lax.ppermute(x, 'z', perm)]
    reduce_scatter x1 -> x0, waiting for transfers between devices: 40.6 us -> none  [shards(): lax.psum_scatter(partial_rows.astype(jnp.bfloat16), 'expert', scatter_dim...]
    unnamed x1 -> x0, blocking collectives: 18.4 us -> none
    select_n x8, other arithmetic: 10.7 us -> 24.6 us  [the longest x5 21.8 us: by_core(): return (jnp.where(first, own, other), jnp.where(first, other, own))]
    dot_general x9 -> x20, matrix products: 81.5 us -> 93.6 us  [the longest x1 33.7 us: shards(): pre = jnp.einsum('rd,fd->rf', routed, w_in, preferred_element_type=F32)]
  transfers between devices with their start and end apart: 5 -> 49, of which waited for: 5 -> 26; matrix products, arithmetic and copies ran while one was open for 2% -> 21% of each run, Pallas kernels for 0% -> 0%
where the time goes in v1:
time: 582 us; the launch traced here: 575 us
  waiting for transfers between devices  327 us (56%)
  starting transfers between devices  106 us (18%)
  matrix products  93.6 us (16%)
  other arithmetic  37.3 us (6%)
  local copies, waits for them, and re-layouts  8.75 us (2%)
    ppermute x33, waiting for transfers between devices, shift_z(): return lax.ppermute(x, 'z', perm)  214 us
    ppermute x9, waiting for transfers between devices, to_expert(): return lax.ppermute(x, 'expert', [(i, i ^ k) for i in range(n)])  113 us
    ppermute x33, starting transfers between devices, shift_z(): return lax.ppermute(x, 'z', perm)  91.4 us
    dot_general x1, matrix products, shards(): pre = jnp.einsum('rd,fd->rf', routed, w_in, preferred_element_type=F32)  33.7 us
    dot_general x4, matrix products, shards(): expert_out = expert_out + jnp.dot(piece, w, preferred_element_type=F32)  24.7 us
    select_n x5, other arithmetic, by_core(): return (jnp.where(first, own, other), jnp.where(first, other, own))  21.8 us
    dot_general x4, matrix products, projected_for(): jnp.einsum('std,df->stf', block, w_out, preferred_element_type=F32)  17.2 us
    ppermute x9, starting transfers between devices, to_expert(): return lax.ppermute(x, 'expert', [(i, i ^ k) for i in range(n)])  13.9 us
  transfers between devices with their start and end apart: 49, of which 26 were waited for; matrix products, arithmetic and copies ran while one was open for 21% of the time, Pallas kernels for 0%

profile of v1, /device:TPU:0, one launch (start us, length us, event | category | flops | bytes accessed | tf_op | source)
XLA Modules:
  0.0 574.9 jit_solution(16542050720718807832)
XLA Ops:
  1.3 1.5 copy.50
  2.8 3.3 fusion.94
  7.9 4.6 collective-permute-start.6
  12.5 3.3 collective-permute-start.10
  15.8 1.8 collective-permute-start.8
  19.1 1.9 collective-permute-start.5
  23.8 3.8 collective-permute-done.5
  27.7 5.7 collective-permute-done.7
  33.3 4.7 collective-permute-done.9
  39.5 4.3 fusion.38
  43.9 3.3 multiply_reduce_fusion
  49.4 9.4 %collective-permute-start.12 = (bf16[256,2048]{1,0:T(8,128)(2,1)S(1)}, bf16[256,2048]{1,0:T(8,128)(2,1)}, u32[]{:S(2)}, u32[]{:S(2)}) collective-permute-start(bf16[256,2048]{1,0:T(8,128)(2,1)S(1)} %copy.40), channel_id=1, source_target_pairs={{0,8},{8,16},{16,24},{1,9},{9,17},{17,25},{2,10},{10,18},{18,26},{... | collective-permute-start | bytes 3145736 | tf_op jit(solution)/shard_map/ppermute | solution.py:21
  58.8 21.0 %collective-permute-done.13 = bf16[256,2048]{1,0:T(8,128)(2,1)} collective-permute-done((bf16[256,2048]{1,0:T(8,128)(2,1)S(1)}, bf16[256,2048]{1,0:T(8,128)(2,1)}, u32[]{:S(2)}, u32[]{:S(2)}) %collective-permute-start.13) | collective-permute-done | bytes 1048608 | tf_op jit(solution)/shard_map/ppermute | solution.py:21
  81.0 5.5 collective-permute-start.16
  88.8 18.1 %collective-permute-done.14 = bf16[256,2048]{1,0:T(8,128)(2,1)} collective-permute-done((bf16[256,2048]{1,0:T(8,128)(2,1)}, bf16[256,2048]{1,0:T(8,128)(2,1)}, u32[]{:S(2)}, u32[]{:S(2)}) %collective-permute-start.14) | collective-permute-done | bytes 1048608 | tf_op jit(solution)/shard_map/ppermute | solution.py:21
  108.2 4.8 collective-permute-start.17
  114.4 2.3 broadcast_select_fusion.7
  116.7 16.4 %collective-permute-done.15 = bf16[256,2048]{1,0:T(8,128)(2,1)S(1)} collective-permute-done((bf16[256,2048]{1,0:T(8,128)(2,1)}, bf16[256,2048]{1,0:T(8,128)(2,1)S(1)}, u32[]{:S(2)}, u32[]{:S(2)}) %collective-permute-start.15) | collective-permute-done | bytes 1048608 | tf_op jit(solution)/shard_map/ppermute | solution.py:21
  136.3 4.0 convolution_convert_fusion.7
  140.3 2.5 collective-permute-start.19
  142.8 4.0 convolution_convert_fusion.6
  147.3 3.9 convolution_convert_fusion.5
  151.7 1.6 constant_dynamic-slice_fusion.8
  153.4 2.4 collective-permute-start
  155.8 5.8 %collective-permute-done = bf16[64,1536]{1,0:T(8,128)(2,1)S(1)} collective-permute-done((bf16[64,1536]{1,0:T(8,128)(2,1)S(1)}, bf16[64,1536]{1,0:T(8,128)(2,1)S(1)}, u32[]{:S(2)}, u32[]{:S(2)}) %collective-permute-start) | collective-permute-done | bytes 196640 | tf_op jit(solution)/shard_map/ppermute | solution.py:21
  161.7 3.6 collective-permute-start.1
  165.3 7.7 %collective-permute-done.1 = bf16[64,1536]{1,0:T(8,128)(2,1)S(1)} collective-permute-done((bf16[64,1536]{1,0:T(8,128)(2,1)S(1)}, bf16[64,1536]{1,0:T(8,128)(2,1)S(1)}, u32[]{:S(2)}, u32[]{:S(2)}) %collective-permute-start.1) | collective-permute-done | bytes 196640 | tf_op jit(solution)/shard_map/ppermute | solution.py:21
  173.1 5.6 collective-permute-done.2
  178.7 5.3 add_convert_fusion.1
  185.9 4.6 collective-permute-start.25
  191.3 14.5 %collective-permute-done.22 = f32[1,64,4]{1,2,0:T(4,128)S(1)} collective-permute-done((f32[1,64,4]{1,2,0:T(4,128)S(1)}, f32[1,64,4]{1,2,0:T(4,128)S(1)}, u32[]{:S(2)}, u32[]{:S(2)}) %collective-permute-start.22) | collective-permute-done | bytes 1056 | tf_op jit(solution)/shard_map/ppermute | solution.py:21
  205.8 3.7 collective-permute-start.24
  212.2 4.6 collective-permute-start.29
  217.2 15.6 %collective-permute-done.27 = bf16[4,64,1536]{2,1,0:T(8,128)(2,1)S(1)} collective-permute-done((bf16[4,64,1536]{2,1,0:T(8,128)(2,1)S(1)}, bf16[4,64,1536]{2,1,0:T(8,128)(2,1)S(1)}, u32[]{:S(2)}, u32[]{:S(2)}) %collective-permute-start.27) | collective-permute-done | bytes 786464 | tf_op jit(solution)/shard_map/ppermute | solution.py:21
  234.1 4.8 collective-permute-start.30
  239.0 8.4 %broadcast_select_fusion.5 = (bf16[576,6144]{1,0:T(8,128)(2,1)}, bf16[576,6144]{1,0:T(8,128)(2,1)}) fusion(bf16[576,6144]{1,0:T(8,128)(2,1)} %collective-permute-done.34, pred[]{:T(512)S(6)} %eq.62, bf16[1,6144,576]{1,2,0:T(8,128)(2,1)S(1)} %bitcast.225), kind=kLoop, calls=%fused_computation.22 | loop fusion | flops 7077888 | bytes 28311552 | tf_op jit(solution)/shard_map/jit(_where)/select_n | solution.py:31
  247.4 6.4 %collective-permute-done.28 = bf16[4,64,1536]{2,1,0:T(8,128)(2,1)S(1)} collective-permute-done((bf16[4,64,1536]{2,1,0:T(8,128)(2,1)S(1)}, bf16[4,64,1536]{2,1,0:T(8,128)(2,1)S(1)}, u32[]{:S(2)}, u32[]{:S(2)}) %collective-permute-start.28) | collective-permute-done | bytes 786464 | tf_op jit(solution)/shard_map/ppermute | solution.py:21
  258.0 1.5 collective-permute-start.31
  260.8 1.5 collective-permute-start.32
  264.2 5.3 broadcast_select_fusion.3
  270.7 41.5 %collective-permute-done.31 = bf16[4,48,6144]{2,1,0:T(8,128)(2,1)S(1)} collective-permute-done((bf16[4,48,6144]{2,1,0:T(8,128)(2,1)S(1)}, bf16[4,48,6144]{2,1,0:T(8,128)(2,1)S(1)}, u32[]{:S(2)}, u32[]{:S(2)}) %collective-permute-start.31) | collective-permute-done | bytes 2359328 | tf_op jit(solution)/shard_map/ppermute | solution.py:26
  312.2 50.5 %collective-permute-done.32 = bf16[4,48,6144]{2,1,0:T(8,128)(2,1)S(1)} collective-permute-done((bf16[4,48,6144]{2,1,0:T(8,128)(2,1)S(1)}, bf16[4,48,6144]{2,1,0:T(8,128)(2,1)S(1)}, u32[]{:S(2)}, u32[]{:S(2)}) %collective-permute-start.32) | collective-permute-done | bytes 2359328 | tf_op jit(solution)/shard_map/ppermute | solution.py:26
  364.0 33.7 %fusion = f32[768,2304]{1,0:T(8,128)S(1)} fusion(bf16[768,6144]{1,0:T(8,128)(2,1)S(1)} %bitcast.220, bf16[576,6144]{1,0:T(8,128)(2,1)} %get-tuple-element.14, bf16[576,6144]{1,0:T(8,128)(2,1)} %get-tuple-element.13, bf16[576,6144]{1,0:T(8,128)(2,1)} %get-tuple-element.12, bf16[576,6144]{1,0:T(8,128)(2,1)} %get-tuple-element.11), kind=kOutput, calls=%fused_computation | convolution fusion | flops 21856518144 | bytes 44826624 | tf_op jit(solution)/shard_map/rd,fd->rf/dot_general | solution.py:194
  400.1 5.1 collective-permute-start.37
  405.2 32.7 %collective-permute-done.38 = bf16[768,1152]{1,0:T(8,128)(2,1)S(1)} collective-permute-done((bf16[768,1152]{1,0:T(8,128)(2,1)S(1)}, bf16[768,1152]{1,0:T(8,128)(2,1)S(1)}, u32[]{:S(2)}, u32[]{:S(2)}) %collective-permute-start.38) | collective-permute-done | bytes 1769504 | tf_op jit(solution)/shard_map/ppermute | solution.py:21
  439.2 6.1 %collective-permute-start.41 = (bf16[768,1152]{1,0:T(8,128)(2,1)S(1)}, bf16[768,1152]{1,0:T(8,128)(2,1)}, u32[]{:S(2)}, u32[]{:S(2)}) collective-permute-start(bf16[768,1152]{1,0:T(8,128)(2,1)S(1)} %collective-permute-done.37), channel_id=1, source_target_pairs={{0,8},{8,16},{16,24},{1,9},{9,17},{17,25},{2,10},{10,18},{18,26},{... | collective-permute-start | bytes 5308424 | tf_op jit(solution)/shard_map/ppermute | solution.py:21
  445.4 5.8 %broadcast_select_fusion.1 = (bf16[4608,768]{1,0:T(8,128)(2,1)S(1)}, bf16[4608,768]{1,0:T(8,128)(2,1)S(1)}) fusion(bf16[4608,768]{1,0:T(8,128)(2,1)} %collective-permute-done.36, pred[]{:T(512)S(6)} %eq.62, bf16[1,4608,768]{2,1,0:T(8,128)(2,1)} %param.23), kind=kLoop, calls=%fused_computation.18 | loop fusion | flops 7077888 | bytes 28311552 | tf_op jit(solution)/shard_map/jit(_where)/select_n | solution.py:31
  451.2 25.7 %collective-permute-done.39 = bf16[768,1152]{1,0:T(8,128)(2,1)} collective-permute-done((bf16[768,1152]{1,0:T(8,128)(2,1)S(1)}, bf16[768,1152]{1,0:T(8,128)(2,1)}, u32[]{:S(2)}, u32[]{:S(2)}) %collective-permute-start.39) | collective-permute-done | bytes 1769504 | tf_op jit(solution)/shard_map/ppermute | solution.py:21
  478.1 1.9 pad_maximum_fusion
  480.1 6.0 %collective-permute-start.42 = (bf16[768,1152]{1,0:T(8,128)(2,1)}, bf16[768,1152]{1,0:T(8,128)(2,1)}, u32[]{:S(2)}, u32[]{:S(2)}) collective-permute-start(bf16[768,1152]{1,0:T(8,128)(2,1)} %collective-permute-done.41), channel_id=1, source_target_pairs={{0,8},{8,16},{16,24},{1,9},{9,17},{17,25},{2,10},{10,18},{18,26},{... | collective-permute-start | bytes 5308424 | tf_op jit(solution)/shard_map/ppermute | solution.py:21
  486.1 4.9 fusion.18
  491.0 6.5 %fusion.14 = f32[768,1536]{1,0:T(8,128)} fusion(bf16[4,1152,1536]{2,1,0:T(8,128)(2,1)S(1)} %bitcast.216, s32[]{:T(128)S(6)} %select_n.221, bf16[768,1152]{1,0:T(8,128)(2,1)} %collective-permute-done.41, bf16[768,1152]{1,0:T(8,128)(2,1)} %collective-permute-done.39, pred[]{:T(512)S(6)} %ge.7), kind=kOutput, calls=%fused_computation.33 | convolution fusion | flops 2718793728 | bytes 11796485 | tf_op jit(solution)/shard_map/dot_general | solution.py:201
  497.4 17.3 %collective-permute-done.40 = bf16[768,1152]{1,0:T(8,128)(2,1)} collective-permute-done((bf16[768,1152]{1,0:T(8,128)(2,1)}, bf16[768,1152]{1,0:T(8,128)(2,1)}, u32[]{:S(2)}, u32[]{:S(2)}) %collective-permute-start.40) | collective-permute-done | bytes 1769504 | tf_op jit(solution)/shard_map/ppermute | solution.py:21
  514.7 6.5 %fusion.16 = f32[768,1536]{1,0:T(8,128)} fusion(bf16[4,1152,1536]{2,1,0:T(8,128)(2,1)S(1)} %bitcast.217, s32[]{:T(128)S(6)} %select_n.222, bf16[768,1152]{1,0:T(8,128)(2,1)S(1)} %collective-permute-done.37, bf16[768,1152]{1,0:T(8,128)(2,1)} %collective-permute-done.40, pred[]{:T(512)S(6)} %ge.6), kind=kOutput, calls=%fused_computation.35 | convolution fusion | flops 2718793728 | bytes 11796485 | tf_op jit(solution)/shard_map/dot_general | solution.py:201
  521.2 6.9 %add_convert_fusion = bf16[768,1536]{1,0:T(8,128)(2,1)S(1)} fusion(f32[768,1536]{1,0:T(8,128)} %fusion.14, f32[768,1536]{1,0:T(8,128)} %fusion.18, f32[768,1536]{1,0:T(8,128)} %fusion.16, bf16[4,1152,1536]{2,1,0:T(8,128)(2,1)S(1)} %bitcast.218, s32[]{:T(128)S(6)} %select_n.220, bf16[768,1152]{1,0:T(8,128)(2,1)} %collective-permute-done.42, ...), kind=kOutput, calls=%fused_computation.27 | convolution fusion | flops 2723512320 | bytes 23592964 | tf_op jit(solution)/shard_map/dot_general | solution.py:201
  529.0 3.2 collective-permute-start.43
  532.2 2.1 collective-permute-start.44
  536.7 9.9 %collective-permute-done.43 = bf16[4,48,1536]{2,1,0:T(8,128)(2,1)S(1)} collective-permute-done((bf16[4,48,1536]{2,1,0:T(8,128)(2,1)}, bf16[4,48,1536]{2,1,0:T(8,128)(2,1)S(1)}, u32[]{:S(2)}, u32[]{:S(2)}) %collective-permute-start.43) | collective-permute-done | bytes 589856 | tf_op jit(solution)/shard_map/ppermute | solution.py:26
  546.7 8.5 %collective-permute-done.44 = bf16[4,48,1536]{2,1,0:T(8,128)(2,1)} collective-permute-done((bf16[4,48,1536]{2,1,0:T(8,128)(2,1)S(1)}, bf16[4,48,1536]{2,1,0:T(8,128)(2,1)}, u32[]{:S(2)}, u32[]{:S(2)}) %collective-permute-start.44) | collective-permute-done | bytes 589856 | tf_op jit(solution)/shard_map/ppermute | solution.py:26
  555.2 2.2 collective-permute-done.45
  557.4 1.5 pad_maximum_fusion.5
  560.4 2.5 collective-permute-start.47
  564.2 3.8 collective-permute-done.46
  568.1 5.3 collective-permute-done.47
  (157 shorter events, 50.1 us)
Async XLA Ops:
  0.0 39.5 %copy-start = (bf16[256,2048]{1,0:T(8,128)(2,1)S(1)}, bf16[256,2048]{1,0:T(8,128)(2,1)}, u32[]{:S(2)}) copy-start(bf16[256,2048]{1,0:T(8,128)(2,1)} %param.14) | copy-start | bytes 3145732
  6.0 11.7 %collective-permute-start.4 = (bf16[16,128,128]{2,1,0:T(8,128)(2,1)}, bf16[16,128,128]{2,1,0:T(8,128)(2,1)}, u32[]{:S(2)}, u32[]{:S(2)}) collective-permute-start(bf16[16,128,128]{2,1,0:T(8,128)(2,1)} %get-tuple-element.62), channel_id=1, source_target_pairs={{0,4},{4,0},{1,5},{5,1},{2,6},{6,2},{3,7},{7,3},{8,12},{12,8},{9,1... | collective-permute-start | bytes 1572872 | tf_op jit(solution)/shard_map/ppermute | solution.py:12
  6.5 1.4 collective-permute-start.3
  6.6 107.8 %collective-permute-start.18 = (bf16[2048,768]{1,0:T(8,128)(2,1)}, bf16[2048,768]{1,0:T(8,128)(2,1)}, u32[]{:S(2)}, u32[]{:S(2)}) collective-permute-start(bf16[2048,768]{1,0:T(8,128)(2,1)} %param.19), channel_id=1, source_target_pairs={{0,4},{4,0},{1,5},{5,1},{2,6},{6,2},{3,7},{7,3},{8,12},{12,8},{9,1... | collective-permute-start | bytes 9437192 | tf_op jit(solution)/shard_map/ppermute | solution.py:12
  7.9 13.1 %collective-permute-start.6 = (f32[16]{0:T(128)S(1)}, f32[16]{0:T(128)S(1)}, u32[]{:S(2)}, u32[]{:S(2)}) collective-permute-start(f32[16]{0:T(128)S(1)} %get-tuple-element.9), channel_id=1, source_target_pairs={{0,8},{8,16},{16,24},{1,9},{9,17},{17,25},{2,10},{10,18},{18,26},{... | collective-permute-start | bytes 200 | tf_op jit(solution)/shard_map/ppermute | solution.py:21
  12.5 9.8 %collective-permute-start.10 = (f32[16]{0:T(128)S(1)}, f32[16]{0:T(128)S(1)}, u32[]{:S(2)}, u32[]{:S(2)}) collective-permute-start(f32[16]{0:T(128)S(1)} %get-tuple-element.9), channel_id=1, source_target_pairs={{0,24},{1,25},{2,26},{3,27},{4,28},{5,29},{6,30},{7,31}} | collective-permute-start | bytes 200 | tf_op jit(solution)/shard_map/ppermute | solution.py:21
  15.8 7.8 %collective-permute-start.8 = (f32[16]{0:T(128)S(1)}, f32[16]{0:T(128)S(1)}, u32[]{:S(2)}, u32[]{:S(2)}) collective-permute-start(f32[16]{0:T(128)S(1)} %get-tuple-element.9), channel_id=1, source_target_pairs={{0,16},{8,24},{1,17},{9,25},{2,18},{10,26},{3,19},{11,27},{4,20},{... | collective-permute-start | bytes 200 | tf_op jit(solution)/shard_map/ppermute | solution.py:21
  19.1 8.6 %collective-permute-start.5 = (bf16[8,128,128]{2,1,0:T(8,128)(2,1)S(1)}, bf16[8,128,128]{2,1,0:T(8,128)(2,1)S(1)}, u32[]{:S(2)}, u32[]{:S(2)}) collective-permute-start(bf16[8,128,128]{2,1,0:T(8,128)(2,1)S(1)} %add_convert_fusion.3), channel_id=1, source_target_pairs={{0,8},{8,16},{16,24},{1,9},{9,17},{17,25},{2,10},{10,18},{18,26},{... | collective-permute-start | bytes 786440 | tf_op jit(solution)/shard_map/ppermute | solution.py:21
  21.0 12.3 %collective-permute-start.7 = (bf16[8,128,128]{2,1,0:T(8,128)(2,1)S(1)}, bf16[8,128,128]{2,1,0:T(8,128)(2,1)S(1)}, u32[]{:S(2)}, u32[]{:S(2)}) collective-permute-start(bf16[8,128,128]{2,1,0:T(8,128)(2,1)S(1)} %add_convert_fusion.3), channel_id=1, source_target_pairs={{0,16},{8,24},{1,17},{9,25},{2,18},{10,26},{3,19},{11,27},{4,20},{... | collective-permute-start | bytes 786440 | tf_op jit(solution)/shard_map/ppermute | solution.py:21
  22.4 15.7 %collective-permute-start.9 = (bf16[8,128,128]{2,1,0:T(8,128)(2,1)S(1)}, bf16[8,128,128]{2,1,0:T(8,128)(2,1)S(1)}, u32[]{:S(2)}, u32[]{:S(2)}) collective-permute-start(bf16[8,128,128]{2,1,0:T(8,128)(2,1)S(1)} %add_convert_fusion.3), channel_id=1, source_target_pairs={{0,24},{1,25},{2,26},{3,27},{4,28},{5,29},{6,30},{7,31}} | collective-permute-start | bytes 786440 | tf_op jit(solution)/shard_map/ppermute | solution.py:21
  39.4 4.4 collective-permute-start.11
  47.1 39.5 %copy-start.6 = (bf16[64,6144]{1,0:T(8,128)(2,1)S(1)}, bf16[64,6144]{1,0:T(8,128)(2,1)}, u32[]{:S(2)}) copy-start(bf16[64,6144]{1,0:T(8,128)(2,1)} %param.13) | copy-start | bytes 2359300
  48.1 31.7 %collective-permute-start.13 = (bf16[256,2048]{1,0:T(8,128)(2,1)S(1)}, bf16[256,2048]{1,0:T(8,128)(2,1)}, u32[]{:S(2)}, u32[]{:S(2)}) collective-permute-start(bf16[256,2048]{1,0:T(8,128)(2,1)S(1)} %copy.40), channel_id=1, source_target_pairs={{8,0},{16,8},{24,16},{9,1},{17,9},{25,17},{10,2},{18,10},{26,18},{... | collective-permute-start | bytes 3145736 | tf_op jit(solution)/shard_map/ppermute | solution.py:21
  49.4 31.7 %collective-permute-start.12 = (bf16[256,2048]{1,0:T(8,128)(2,1)S(1)}, bf16[256,2048]{1,0:T(8,128)(2,1)}, u32[]{:S(2)}, u32[]{:S(2)}) collective-permute-start(bf16[256,2048]{1,0:T(8,128)(2,1)S(1)} %copy.40), channel_id=1, source_target_pairs={{0,8},{8,16},{16,24},{1,9},{9,17},{17,25},{2,10},{10,18},{18,26},{... | collective-permute-start | bytes 3145736 | tf_op jit(solution)/shard_map/ppermute | solution.py:21
  79.7 27.2 %collective-permute-start.14 = (bf16[256,2048]{1,0:T(8,128)(2,1)}, bf16[256,2048]{1,0:T(8,128)(2,1)}, u32[]{:S(2)}, u32[]{:S(2)}) collective-permute-start(bf16[256,2048]{1,0:T(8,128)(2,1)} %collective-permute-done.13), channel_id=1, source_target_pairs={{8,0},{16,8},{24,16},{9,1},{17,9},{25,17},{10,2},{18,10},{26,18},{... | collective-permute-start | bytes 3145736 | tf_op jit(solution)/shard_map/ppermute | solution.py:21
  81.0 27.2 %collective-permute-start.16 = (bf16[256,2048]{1,0:T(8,128)(2,1)}, bf16[256,2048]{1,0:T(8,128)(2,1)}, u32[]{:S(2)}, u32[]{:S(2)}) collective-permute-start(bf16[256,2048]{1,0:T(8,128)(2,1)} %collective-permute-done.12), channel_id=1, source_target_pairs={{0,8},{8,16},{16,24},{1,9},{9,17},{17,25},{2,10},{10,18},{18,26},{... | collective-permute-start | bytes 3145736 | tf_op jit(solution)/shard_map/ppermute | solution.py:21
  86.6 152.4 %collective-permute-start.34 = (bf16[576,6144]{1,0:T(8,128)(2,1)}, bf16[576,6144]{1,0:T(8,128)(2,1)}, u32[]{:S(2)}, u32[]{:S(2)}) collective-permute-start(bf16[576,6144]{1,0:T(8,128)(2,1)} %bitcast.223), channel_id=1, source_target_pairs={{0,4},{4,0},{1,5},{5,1},{2,6},{6,2},{3,7},{7,3},{8,12},{12,8},{9,1... | collective-permute-start | bytes 21233672 | tf_op jit(solution)/shard_map/ppermute | solution.py:12
  88.8 25.6 %copy-start.3 = (bf16[2048,768]{1,0:T(8,128)(2,1)S(1)}, bf16[2048,768]{1,0:T(8,128)(2,1)}, u32[]{:S(2)}) copy-start(bf16[2048,768]{1,0:T(8,128)(2,1)} %param.19) | copy-start | bytes 9437188
  106.9 26.2 %collective-permute-start.15 = (bf16[256,2048]{1,0:T(8,128)(2,1)}, bf16[256,2048]{1,0:T(8,128)(2,1)S(1)}, u32[]{:S(2)}, u32[]{:S(2)}) collective-permute-start(bf16[256,2048]{1,0:T(8,128)(2,1)} %collective-permute-done.14), channel_id=1, source_target_pairs={{8,0},{16,8},{24,16},{9,1},{17,9},{25,17},{10,2},{18,10},{26,18},{... | collective-permute-start | bytes 3145736 | tf_op jit(solution)/shard_map/ppermute | solution.py:21
  108.2 26.2 %collective-permute-start.17 = (bf16[256,2048]{1,0:T(8,128)(2,1)}, bf16[256,2048]{1,0:T(8,128)(2,1)S(1)}, u32[]{:S(2)}, u32[]{:S(2)}) collective-permute-start(bf16[256,2048]{1,0:T(8,128)(2,1)} %collective-permute-done.16), channel_id=1, source_target_pairs={{0,8},{8,16},{16,24},{1,9},{9,17},{17,25},{2,10},{10,18},{18,26},{... | collective-permute-start | bytes 3145736 | tf_op jit(solution)/shard_map/ppermute | solution.py:21
  116.7 30.6 %copy-start.4 = (bf16[2048,768]{1,0:T(8,128)(2,1)}, bf16[2048,768]{1,0:T(8,128)(2,1)S(1)}, u32[]{:S(2)}) copy-start(bf16[2048,768]{1,0:T(8,128)(2,1)S(1)} %get-tuple-element.17) | copy-start | bytes 9437188
  116.7 30.6 %copy-start.5 = (bf16[2048,768]{1,0:T(8,128)(2,1)}, bf16[2048,768]{1,0:T(8,128)(2,1)S(1)}, u32[]{:S(2)}) copy-start(bf16[2048,768]{1,0:T(8,128)(2,1)S(1)} %get-tuple-element.18) | copy-start | bytes 9437188
  136.3 10.9 %copy-start.2 = (bf16[4,4,64,2048]{3,2,1,0:T(8,128)(2,1)}, bf16[4,4,64,2048]{3,2,1,0:T(8,128)(2,1)S(1)}, u32[]{:S(2)}) copy-start(bf16[4,4,64,2048]{3,2,1,0:T(8,128)(2,1)S(1)} %pad_maximum_fusion.2) | copy-start | bytes 12582916
  140.3 38.4 %collective-permute-start.19 = (bf16[4,64,1536]{2,1,0:T(8,128)(2,1)}, bf16[4,64,1536]{2,1,0:T(8,128)(2,1)S(1)}, u32[]{:S(2)}, u32[]{:S(2)}) collective-permute-start(bf16[4,64,1536]{2,1,0:T(8,128)(2,1)} %convolution_convert_fusion.7), channel_id=1, source_target_pairs={{0,3},{1,2},{2,1},{3,0},{4,7},{5,6},{6,5},{7,4},{8,11},{9,10},{10,... | collective-permute-start | bytes 2359304 | tf_op jit(solution)/shard_map/ppermute | solution.py:26
  146.7 31.9 %collective-permute-start.20 = (bf16[4,64,1536]{2,1,0:T(8,128)(2,1)}, bf16[4,64,1536]{2,1,0:T(8,128)(2,1)S(1)}, u32[]{:S(2)}, u32[]{:S(2)}) collective-permute-start(bf16[4,64,1536]{2,1,0:T(8,128)(2,1)} %convolution_convert_fusion.6), channel_id=1, source_target_pairs={{0,2},{1,3},{2,0},{3,1},{4,6},{5,7},{6,4},{7,5},{8,10},{9,11},{10,... | collective-permute-start | bytes 2359304 | tf_op jit(solution)/shard_map/ppermute | solution.py:26
  151.2 27.5 %collective-permute-start.21 = (bf16[4,64,1536]{2,1,0:T(8,128)(2,1)}, bf16[4,64,1536]{2,1,0:T(8,128)(2,1)}, u32[]{:S(2)}, u32[]{:S(2)}) collective-permute-start(bf16[4,64,1536]{2,1,0:T(8,128)(2,1)} %convolution_convert_fusion.5), channel_id=1, source_target_pairs={{0,1},{1,0},{2,3},{3,2},{4,5},{5,4},{6,7},{7,6},{8,9},{9,8},{10,11... | collective-permute-start | bytes 2359304 | tf_op jit(solution)/shard_map/ppermute | solution.py:26
  153.4 8.3 %collective-permute-start = (bf16[64,1536]{1,0:T(8,128)(2,1)S(1)}, bf16[64,1536]{1,0:T(8,128)(2,1)S(1)}, u32[]{:S(2)}, u32[]{:S(2)}) collective-permute-start(bf16[64,1536]{1,0:T(8,128)(2,1)S(1)} %bitcast.248), channel_id=1, source_target_pairs={{0,8},{8,16},{16,24},{24,0},{1,9},{9,17},{17,25},{25,1},{2,10},{10... | collective-permute-start | bytes 589832 | tf_op jit(solution)/shard_map/ppermute | solution.py:21
  161.7 11.3 %collective-permute-start.1 = (bf16[64,1536]{1,0:T(8,128)(2,1)S(1)}, bf16[64,1536]{1,0:T(8,128)(2,1)S(1)}, u32[]{:S(2)}, u32[]{:S(2)}) collective-permute-start(bf16[64,1536]{1,0:T(8,128)(2,1)S(1)} %bitcast.247), channel_id=1, source_target_pairs={{0,16},{8,24},{16,0},{24,8},{1,17},{9,25},{17,1},{25,9},{2,18},{10... | collective-permute-start | bytes 589832 | tf_op jit(solution)/shard_map/ppermute | solution.py:21
  173.0 5.7 collective-permute-start.2
  178.7 30.9 %slice-start.2 = ((s8[7077888]{0:T(1024)(128)(4,1)}), s8[4194304]{0:T(1024)(128)(4,1)S(1)}, s32[]{:S(2)}) async-start(s8[7077888]{0:T(1024)(128)(4,1)} %bitcast.226), calls=%async_computation.2 | async-start | bytes 8388608
  178.7 60.3 %slice-start = ((s8[7077888]{0:T(1024)(128)(4,1)}), s8[4194304]{0:T(1024)(128)(4,1)S(1)}, s32[]{:S(2)}) async-start(s8[7077888]{0:T(1024)(128)(4,1)} %bitcast.224), calls=%async_computation | async-start | bytes 8388608
  178.7 30.8 %slice-start.3 = ((s8[7077888]{0:T(1024)(128)(4,1)}), s8[2883584]{0:T(1024)(128)(4,1)S(1)}, s32[]{:S(2)}) async-start(s8[7077888]{0:T(1024)(128)(4,1)} %bitcast.226), calls=%async_computation.3 | async-start | bytes 5767168
  178.7 60.3 %slice-start.1 = ((s8[7077888]{0:T(1024)(128)(4,1)}), s8[2883584]{0:T(1024)(128)(4,1)S(1)}, s32[]{:S(2)}) async-start(s8[7077888]{0:T(1024)(128)(4,1)} %bitcast.224), calls=%async_computation.1 | async-start | bytes 5767168
  184.0 6.5 %copy-start.7 = (s32[64,2]{0,1:T(2,128)S(1)}, s32[64,2]{0,1:T(2,128)}, u32[]{:S(2)}) copy-start(s32[64,2]{0,1:T(2,128)} %param.24) | copy-start | bytes 1540
  184.1 6.5 %copy-start.8 = (f32[64,2]{0,1:T(2,128)S(1)}, f32[64,2]{0,1:T(2,128)}, u32[]{:S(2)}) copy-start(f32[64,2]{0,1:T(2,128)} %param.25) | copy-start | bytes 1540
  184.5 26.5 %collective-permute-start.26 = (bf16[4,64,1536]{2,1,0:T(8,128)(2,1)S(1)}, bf16[4,64,1536]{2,1,0:T(8,128)(2,1)S(1)}, u32[]{:S(2)}, u32[]{:S(2)}) collective-permute-start(bf16[4,64,1536]{2,1,0:T(8,128)(2,1)S(1)} %get-tuple-element.36), channel_id=1, source_target_pairs={{8,0},{16,8},{24,16},{9,1},{17,9},{25,17},{10,2},{18,10},{26,18},{... | collective-permute-start | bytes 2359304 | tf_op jit(solution)/shard_map/ppermute | solution.py:21
  185.9 26.4 %collective-permute-start.25 = (bf16[4,64,1536]{2,1,0:T(8,128)(2,1)S(1)}, bf16[4,64,1536]{2,1,0:T(8,128)(2,1)S(1)}, u32[]{:S(2)}, u32[]{:S(2)}) collective-permute-start(bf16[4,64,1536]{2,1,0:T(8,128)(2,1)S(1)} %get-tuple-element.36), channel_id=1, source_target_pairs={{0,8},{8,16},{16,24},{1,9},{9,17},{17,25},{2,10},{10,18},{18,26},{... | collective-permute-start | bytes 2359304 | tf_op jit(solution)/shard_map/ppermute | solution.py:21
  190.5 15.3 %collective-permute-start.22 = (f32[1,64,4]{1,2,0:T(4,128)S(1)}, f32[1,64,4]{1,2,0:T(4,128)S(1)}, u32[]{:S(2)}, u32[]{:S(2)}) collective-permute-start(f32[1,64,4]{1,2,0:T(4,128)S(1)} %get-tuple-element.60), channel_id=1, source_target_pairs={{0,8},{8,16},{16,24},{24,0},{1,9},{9,17},{17,25},{25,1},{2,10},{10... | collective-permute-start | bytes 3080 | tf_op jit(solution)/shard_map/ppermute | solution.py:21
  190.6 19.0 %collective-permute-start.23 = (f32[1,64,4]{1,2,0:T(4,128)S(1)}, f32[1,64,4]{1,2,0:T(4,128)S(1)}, u32[]{:S(2)}, u32[]{:S(2)}) collective-permute-start(f32[1,64,4]{1,2,0:T(4,128)S(1)} %get-tuple-element.60), channel_id=1, source_target_pairs={{0,16},{8,24},{16,0},{24,8},{1,17},{9,25},{17,1},{25,9},{2,18},{10... | collective-permute-start | bytes 3080 | tf_op jit(solution)/shard_map/ppermute | solution.py:21
  205.8 5.0 collective-permute-start.24
  209.6 54.6 %collective-permute-start.35 = (bf16[576,6144]{1,0:T(8,128)(2,1)S(1)}, bf16[576,6144]{1,0:T(8,128)(2,1)S(1)}, u32[]{:S(2)}, u32[]{:S(2)}) collective-permute-start(bf16[576,6144]{1,0:T(8,128)(2,1)S(1)} %bitcast.228), channel_id=1, source_target_pairs={{0,4},{4,0},{1,5},{5,1},{2,6},{6,2},{3,7},{7,3},{8,12},{12,8},{9,1... | collective-permute-start | bytes 21233672 | tf_op jit(solution)/shard_map/ppermute | solution.py:12
  210.9 234.5 %collective-permute-start.36 = (bf16[4608,768]{1,0:T(8,128)(2,1)}, bf16[4608,768]{1,0:T(8,128)(2,1)}, u32[]{:S(2)}, u32[]{:S(2)}) collective-permute-start(bf16[4608,768]{1,0:T(8,128)(2,1)} %bitcast.65), channel_id=1, source_target_pairs={{0,4},{4,0},{1,5},{5,1},{2,6},{6,2},{3,7},{7,3},{8,12},{12,8},{9,1... | collective-permute-start | bytes 21233672 | tf_op jit(solution)/shard_map/ppermute | solution.py:12
  210.9 21.8 %collective-permute-start.27 = (bf16[4,64,1536]{2,1,0:T(8,128)(2,1)S(1)}, bf16[4,64,1536]{2,1,0:T(8,128)(2,1)S(1)}, u32[]{:S(2)}, u32[]{:S(2)}) collective-permute-start(bf16[4,64,1536]{2,1,0:T(8,128)(2,1)S(1)} %collective-permute-done.26), channel_id=1, source_target_pairs={{8,0},{16,8},{24,16},{9,1},{17,9},{25,17},{10,2},{18,10},{26,18},{... | collective-permute-start | bytes 2359304 | tf_op jit(solution)/shard_map/ppermute | solution.py:21
  212.2 21.8 %collective-permute-start.29 = (bf16[4,64,1536]{2,1,0:T(8,128)(2,1)S(1)}, bf16[4,64,1536]{2,1,0:T(8,128)(2,1)S(1)}, u32[]{:S(2)}, u32[]{:S(2)}) collective-permute-start(bf16[4,64,1536]{2,1,0:T(8,128)(2,1)S(1)} %collective-permute-done.25), channel_id=1, source_target_pairs={{0,8},{8,16},{16,24},{1,9},{9,17},{17,25},{2,10},{10,18},{18,26},{... | collective-permute-start | bytes 2359304 | tf_op jit(solution)/shard_map/ppermute | solution.py:21
  232.8 21.0 %collective-permute-start.28 = (bf16[4,64,1536]{2,1,0:T(8,128)(2,1)S(1)}, bf16[4,64,1536]{2,1,0:T(8,128)(2,1)S(1)}, u32[]{:S(2)}, u32[]{:S(2)}) collective-permute-start(bf16[4,64,1536]{2,1,0:T(8,128)(2,1)S(1)} %collective-permute-done.27), channel_id=1, source_target_pairs={{8,0},{16,8},{24,16},{9,1},{17,9},{25,17},{10,2},{18,10},{26,18},{... | collective-permute-start | bytes 2359304 | tf_op jit(solution)/shard_map/ppermute | solution.py:21
  234.1 20.9 %collective-permute-start.30 = (bf16[4,64,1536]{2,1,0:T(8,128)(2,1)S(1)}, bf16[4,64,1536]{2,1,0:T(8,128)(2,1)S(1)}, u32[]{:S(2)}, u32[]{:S(2)}) collective-permute-start(bf16[4,64,1536]{2,1,0:T(8,128)(2,1)S(1)} %collective-permute-done.29), channel_id=1, source_target_pairs={{0,8},{8,16},{16,24},{1,9},{9,17},{17,25},{2,10},{10,18},{18,26},{... | collective-permute-start | bytes 2359304 | tf_op jit(solution)/shard_map/ppermute | solution.py:21
  255.6 1.2 copy-start.9
  258.0 54.3 %collective-permute-start.31 = (bf16[4,48,6144]{2,1,0:T(8,128)(2,1)S(1)}, bf16[4,48,6144]{2,1,0:T(8,128)(2,1)S(1)}, u32[]{:S(2)}, u32[]{:S(2)}) collective-permute-start(bf16[4,48,6144]{2,1,0:T(8,128)(2,1)S(1)} %convolution_convert_fusion.2), channel_id=1, source_target_pairs={{0,1},{1,0},{2,3},{3,2},{4,5},{5,4},{6,7},{7,6},{8,9},{9,8},{10,11... | collective-permute-start | bytes 7077896 | tf_op jit(solution)/shard_map/ppermute | solution.py:26
  260.8 102.0 %collective-permute-start.32 = (bf16[4,48,6144]{2,1,0:T(8,128)(2,1)S(1)}, bf16[4,48,6144]{2,1,0:T(8,128)(2,1)S(1)}, u32[]{:S(2)}, u32[]{:S(2)}) collective-permute-start(bf16[4,48,6144]{2,1,0:T(8,128)(2,1)S(1)} %convolution_convert_fusion.1), channel_id=1, source_target_pairs={{0,2},{1,3},{2,0},{3,1},{4,6},{5,7},{6,4},{7,5},{8,10},{9,11},{10,... | collective-permute-start | bytes 7077896 | tf_op jit(solution)/shard_map/ppermute | solution.py:26
  263.5 99.2 %collective-permute-start.33 = (bf16[4,48,6144]{2,1,0:T(8,128)(2,1)S(1)}, bf16[4,48,6144]{2,1,0:T(8,128)(2,1)S(1)}, u32[]{:S(2)}, u32[]{:S(2)}) collective-permute-start(bf16[4,48,6144]{2,1,0:T(8,128)(2,1)S(1)} %convolution_convert_fusion), channel_id=1, source_target_pairs={{0,3},{1,2},{2,1},{3,0},{4,7},{5,6},{6,5},{7,4},{8,11},{9,10},{10,... | collective-permute-start | bytes 7077896 | tf_op jit(solution)/shard_map/ppermute | solution.py:26
  398.8 39.1 %collective-permute-start.38 = (bf16[768,1152]{1,0:T(8,128)(2,1)S(1)}, bf16[768,1152]{1,0:T(8,128)(2,1)S(1)}, u32[]{:S(2)}, u32[]{:S(2)}) collective-permute-start(bf16[768,1152]{1,0:T(8,128)(2,1)S(1)} %fusion.12), channel_id=1, source_target_pairs={{8,0},{16,8},{24,16},{9,1},{17,9},{25,17},{10,2},{18,10},{26,18},{... | collective-permute-start | bytes 5308424 | tf_op jit(solution)/shard_map/ppermute | solution.py:21
  400.1 39.1 %collective-permute-start.37 = (bf16[768,1152]{1,0:T(8,128)(2,1)S(1)}, bf16[768,1152]{1,0:T(8,128)(2,1)S(1)}, u32[]{:S(2)}, u32[]{:S(2)}) collective-permute-start(bf16[768,1152]{1,0:T(8,128)(2,1)S(1)} %fusion.12), channel_id=1, source_target_pairs={{0,8},{8,16},{16,24},{1,9},{9,17},{17,25},{2,10},{10,18},{18,26},{... | collective-permute-start | bytes 5308424 | tf_op jit(solution)/shard_map/ppermute | solution.py:21
  437.9 38.9 %collective-permute-start.39 = (bf16[768,1152]{1,0:T(8,128)(2,1)S(1)}, bf16[768,1152]{1,0:T(8,128)(2,1)}, u32[]{:S(2)}, u32[]{:S(2)}) collective-permute-start(bf16[768,1152]{1,0:T(8,128)(2,1)S(1)} %collective-permute-done.38), channel_id=1, source_target_pairs={{8,0},{16,8},{24,16},{9,1},{17,9},{25,17},{10,2},{18,10},{26,18},{... | collective-permute-start | bytes 5308424 | tf_op jit(solution)/shard_map/ppermute | solution.py:21
  439.2 40.8 %collective-permute-start.41 = (bf16[768,1152]{1,0:T(8,128)(2,1)S(1)}, bf16[768,1152]{1,0:T(8,128)(2,1)}, u32[]{:S(2)}, u32[]{:S(2)}) collective-permute-start(bf16[768,1152]{1,0:T(8,128)(2,1)S(1)} %collective-permute-done.37), channel_id=1, source_target_pairs={{0,8},{8,16},{16,24},{1,9},{9,17},{17,25},{2,10},{10,18},{18,26},{... | collective-permute-start | bytes 5308424 | tf_op jit(solution)/shard_map/ppermute | solution.py:21
  476.9 37.9 %collective-permute-start.40 = (bf16[768,1152]{1,0:T(8,128)(2,1)}, bf16[768,1152]{1,0:T(8,128)(2,1)}, u32[]{:S(2)}, u32[]{:S(2)}) collective-permute-start(bf16[768,1152]{1,0:T(8,128)(2,1)} %collective-permute-done.39), channel_id=1, source_target_pairs={{8,0},{16,8},{24,16},{9,1},{17,9},{25,17},{10,2},{18,10},{26,18},{... | collective-permute-start | bytes 5308424 | tf_op jit(solution)/shard_map/ppermute | solution.py:21
  480.1 41.2 %collective-permute-start.42 = (bf16[768,1152]{1,0:T(8,128)(2,1)}, bf16[768,1152]{1,0:T(8,128)(2,1)}, u32[]{:S(2)}, u32[]{:S(2)}) collective-permute-start(bf16[768,1152]{1,0:T(8,128)(2,1)} %collective-permute-done.41), channel_id=1, source_target_pairs={{0,8},{8,16},{16,24},{1,9},{9,17},{17,25},{2,10},{10,18},{18,26},{... | collective-permute-start | bytes 5308424 | tf_op jit(solution)/shard_map/ppermute | solution.py:21
  529.0 17.6 %collective-permute-start.43 = (bf16[4,48,1536]{2,1,0:T(8,128)(2,1)}, bf16[4,48,1536]{2,1,0:T(8,128)(2,1)S(1)}, u32[]{:S(2)}, u32[]{:S(2)}) collective-permute-start(bf16[4,48,1536]{2,1,0:T(8,128)(2,1)} %bitcast.72), channel_id=1, source_target_pairs={{0,1},{1,0},{2,3},{3,2},{4,5},{5,4},{6,7},{7,6},{8,9},{9,8},{10,11... | collective-permute-start | bytes 1769480 | tf_op jit(solution)/shard_map/ppermute | solution.py:26
  532.2 23.0 %collective-permute-start.44 = (bf16[4,48,1536]{2,1,0:T(8,128)(2,1)S(1)}, bf16[4,48,1536]{2,1,0:T(8,128)(2,1)}, u32[]{:S(2)}, u32[]{:S(2)}) collective-permute-start(bf16[4,48,1536]{2,1,0:T(8,128)(2,1)S(1)} %bitcast.241), channel_id=1, source_target_pairs={{0,2},{1,3},{2,0},{3,1},{4,6},{5,7},{6,4},{7,5},{8,10},{9,11},{10,... | collective-permute-start | bytes 1769480 | tf_op jit(solution)/shard_map/ppermute | solution.py:26
  534.3 23.1 %collective-permute-start.45 = (bf16[4,48,1536]{2,1,0:T(8,128)(2,1)S(1)}, bf16[4,48,1536]{2,1,0:T(8,128)(2,1)}, u32[]{:S(2)}, u32[]{:S(2)}) collective-permute-start(bf16[4,48,1536]{2,1,0:T(8,128)(2,1)S(1)} %bitcast.239), channel_id=1, source_target_pairs={{0,3},{1,2},{2,1},{3,0},{4,7},{5,6},{6,5},{7,4},{8,11},{9,10},{10,... | collective-permute-start | bytes 1769480 | tf_op jit(solution)/shard_map/ppermute | solution.py:26
  559.7 14.7 %copy-start.1 = (bf16[256,2048]{1,0:T(8,128)(2,1)S(1)}, bf16[256,2048]{1,0:T(8,128)(2,1)}, u32[]{:S(2)}) copy-start(bf16[256,2048]{1,0:T(8,128)(2,1)} %param.14) | copy-start | bytes 3145732
  560.3 7.7 %collective-permute-start.46 = (bf16[64,1536]{1,0:T(8,128)(2,1)S(1)}, bf16[64,1536]{1,0:T(8,128)(2,1)S(1)}, u32[]{:S(2)}, u32[]{:S(2)}) collective-permute-start(bf16[64,1536]{1,0:T(8,128)(2,1)S(1)} %get-tuple-element.34), channel_id=1, source_target_pairs={{0,8},{8,16},{16,24},{24,0},{1,9},{9,17},{17,25},{25,1},{2,10},{10... | collective-permute-start | bytes 589832 | tf_op jit(solution)/shard_map/ppermute | solution.py:21
  560.4 12.9 %collective-permute-start.47 = (bf16[64,1536]{1,0:T(8,128)(2,1)S(1)}, bf16[64,1536]{1,0:T(8,128)(2,1)S(1)}, u32[]{:S(2)}, u32[]{:S(2)}) collective-permute-start(bf16[64,1536]{1,0:T(8,128)(2,1)S(1)} %get-tuple-element.33), channel_id=1, source_target_pairs={{0,16},{8,24},{16,0},{24,8},{1,17},{9,25},{17,1},{25,9},{2,18},{10... | collective-permute-start | bytes 589832 | tf_op jit(solution)/shard_map/ppermute | solution.py:21
  562.9 10.5 %collective-permute-start.48 = (bf16[64,1536]{1,0:T(8,128)(2,1)S(1)}, bf16[64,1536]{1,0:T(8,128)(2,1)S(1)}, u32[]{:S(2)}, u32[]{:S(2)}) collective-permute-start(bf16[64,1536]{1,0:T(8,128)(2,1)S(1)} %get-tuple-element.32), channel_id=1, source_target_pairs={{0,24},{8,0},{16,8},{24,16},{1,25},{9,1},{17,9},{25,17},{2,26},{10... | collective-permute-start | bytes 589832 | tf_op jit(solution)/shard_map/ppermute | solution.py:21
